TPU v7x, 128 devices: a whole 4x4x4 slice. The times are simulated.
128 devices in a mesh: grp: 8 (over y, core), dev: 16 (over x, z).
Axes of the slice: x: 4, y: 4, z: 4, core: 2. Of those that a mesh axis runs over, the one named last changes fastest.
Arguments:
- suffix_queries: bfloat16 [16384, 2048], P(('grp', 'dev')), may hold values from -12 to 12
- suffix_keys: bfloat16 [16384, 2048], P(('grp', 'dev')), may hold values from -12 to 12
- suffix_values: bfloat16 [16384, 2048], P(('grp', 'dev')), may hold values from -6 to 6
- layer_input: bfloat16 [16384, 2048], P(('grp', 'dev')), may hold values from -6 to 6
- suffix_lengths: int32 [128, 8], P(('grp', 'dev')), may hold values from 1 to 32, as said below
- request_group: int32 [128, 8], P(('grp', 'dev')), may hold values from 0 to 7, as said below
- prefix_keys: bfloat16 [8, 4096, 2048], P('grp', None, 'dev'), may hold values from -12 to 12
- prefix_values: bfloat16 [8, 4096, 2048], P('grp', None, 'dev'), may hold values from -6 to 6
- up_weight: bfloat16 [2048, 8192], P(None, ('grp', 'dev')), may hold values from -0.125 to 0.125
- up_bias: bfloat16 [8192], P(('grp', 'dev')), may hold values from -3 to 3
- down_weight: bfloat16 [8192, 2048], P(('grp', 'dev')), may hold values from -0.0625 to 0.0625
- down_bias: float32 [2048], replicated, may hold values from -3 to 3
- attn_gain: float32 [2048], replicated, may hold values from 0.5 to 1.5
- attn_shift: float32 [2048], replicated, may hold values from -2 to 2
- out_gain: float32 [2048], replicated, may hold values from 0.5 to 1.5
- out_shift: float32 [2048], replicated, may hold values from -2 to 2
Outputs:
- layer_output: bfloat16 [16384, 2048], P(('grp', 'dev'))
Inputs may be any that keep to these rules, and one draw needn't show every extreme that they name: `suffix_lengths`: each row lists one device's 8 requests in slot order; they fill its 128 slots exactly, and at least one of them has 32 tokens. `request_group`: the 8 requests of one row name every prefix exactly once.
All inputs are finite; a program needn't handle non-finite values.
Results may differ from a plain program's by a relative error of at most 0.014.
Values may be sent and summed in bfloat16 or wider, within the bound.
A program may use at most 128 MiB of HBM per device.

v0:
```python
import math
import jax
import jax.numpy as jnp
from jax import lax
from jax.sharding import PartitionSpec as P

HD = 128
norm_eps = 1e-12


def layer_norm(summed, norm_gain, norm_shift):
    row_mean = jnp.mean(summed, axis=-1, keepdims=True)
    centred = summed - row_mean
    spread = jnp.mean(centred * centred, axis=-1, keepdims=True)
    return centred * lax.rsqrt(spread + norm_eps) * norm_gain + norm_shift


def request_layout(lengths, slot_count):
    end_points = jnp.cumsum(lengths)
    starts = end_points - lengths
    positions = lax.iota(jnp.int32, slot_count)
    member = (positions[:, None] >= starts[None, :]) & (positions[:, None] < end_points[None, :])
    slot_ids = lax.iota(jnp.int32, lengths.shape[0])
    segment = jnp.sum(jnp.where(member, slot_ids[None, :], 0), axis=1)
    return (starts, segment)


def expand_rows(piece_rows, up_matrix, up_offset):
    product = jnp.dot(piece_rows, up_matrix, preferred_element_type=jnp.float32)
    return jax.nn.gelu(product + up_offset.astype(jnp.float32), approximate=True).astype(
        jnp.bfloat16
    )


def attend_prefix(arrived, cache_keys, cache_values):
    sources, row_count, part_width = arrived.shape
    local_heads = part_width // HD
    per_block = math.gcd(sources, max(1, 512 // row_count))
    query_blocks = arrived.reshape(sources // per_block, per_block * row_count, local_heads, HD)
    key_heads = cache_keys.reshape(-1, local_heads, HD)
    value_heads = cache_values.reshape(-1, local_heads, HD)

    def one_block(query_block):
        scores = jnp.einsum(
            "qhd,khd->hqk", query_block, key_heads, preferred_element_type=jnp.float32
        ) * HD ** (-0.5)
        row_top = jnp.max(scores, axis=2).astype(jnp.bfloat16)
        weights = jnp.exp(
            scores - lax.optimization_barrier(row_top).astype(jnp.float32)[:, :, None]
        )
        row_sum = jnp.sum(weights, axis=2)
        mixed_sum = jnp.einsum(
            "hqk,khd->qhd",
            weights.astype(jnp.bfloat16),
            value_heads,
            preferred_element_type=jnp.float32,
        )
        answer = (mixed_sum / row_sum.T[:, :, None]).astype(jnp.bfloat16)
        return (answer.reshape(-1, part_width), row_top.T, row_sum.T.astype(jnp.bfloat16))

    answer, row_top, row_sum = lax.map(one_block, query_blocks)
    return (
        answer.reshape(sources, row_count, part_width),
        row_top.reshape(sources, row_count, local_heads),
        row_sum.reshape(sources, row_count, local_heads),
    )


def attend_suffix(query_rows, key_rows, value_rows, segment, head_count):
    slot_count = query_rows.shape[0]
    query_heads = query_rows.reshape(slot_count, head_count, HD)
    key_heads = key_rows.reshape(slot_count, head_count, HD)
    value_heads = value_rows.reshape(slot_count, head_count, HD)
    scores = jnp.einsum(
        "qhd,khd->hqk", query_heads, key_heads, preferred_element_type=jnp.float32
    ) * HD ** (-0.5)
    positions = lax.iota(jnp.int32, slot_count)
    visible = ((segment[:, None] == segment[None, :]) & (positions[None, :] <= positions[:, None]))[
        None
    ]
    row_top = jnp.max(jnp.where(visible, scores, -jnp.inf), axis=2)
    weights = jnp.where(visible, jnp.exp(scores - row_top[:, :, None]), 0.0)
    row_sum = jnp.sum(weights, axis=2)
    mixed_sum = jnp.einsum(
        "hqk,khd->qhd",
        weights.astype(jnp.bfloat16),
        value_heads,
        preferred_element_type=jnp.float32,
    )
    return (row_top.T, row_sum.T, mixed_sum)


def merge_parts(far_answer, far_top, far_sum, own_top, own_sum, own_mixed):
    far_top = far_top.astype(jnp.float32)
    far_sum = far_sum.astype(jnp.float32)
    joint_top = jnp.maximum(far_top, own_top)
    far_weight = jnp.exp(far_top - joint_top) * far_sum
    own_weight = jnp.exp(own_top - joint_top)
    numerator = (
        far_weight[:, :, None] * far_answer.astype(jnp.float32) + own_weight[:, :, None] * own_mixed
    )
    return numerator / (far_weight + own_weight * own_sum)[:, :, None]


def on_device(
    suffix_queries,
    suffix_keys,
    suffix_values,
    layer_input,
    suffix_lengths,
    request_group,
    prefix_keys,
    prefix_values,
    up_weight,
    up_bias,
    down_weight,
    down_bias,
    attn_gain,
    attn_shift,
    out_gain,
    out_shift,
):
    slot_count, model_width = suffix_queries.shape
    head_count = model_width // HD
    group_count = lax.axis_size("grp")
    column_count = lax.axis_size("dev")
    part_width = model_width // column_count
    local_heads = part_width // HD
    capacity = 2 * slot_count // group_count
    lengths = suffix_lengths[0]
    groups = request_group[0]
    request_total = lengths.shape[0]
    starts, segment = request_layout(lengths, slot_count)
    anchor = jnp.zeros((), jnp.int32)
    padded = jnp.concatenate(
        [suffix_queries, jnp.zeros((capacity, model_width), jnp.bfloat16)], axis=0
    )
    slot_rank = lax.iota(jnp.int32, capacity)
    outgoing = jnp.zeros((group_count, column_count, capacity, part_width), jnp.bfloat16)
    for request in range(request_total):
        taken = lax.dynamic_slice_in_dim(padded, starts[request], capacity, 0)
        taken = jnp.where((slot_rank < lengths[request])[:, None], taken, jnp.zeros_like(taken))
        split_rows = taken.reshape(capacity, column_count, part_width).transpose(1, 0, 2)
        outgoing = lax.dynamic_update_slice(
            outgoing, split_rows[None], (groups[request], anchor, anchor, anchor)
        )
    cache_keys = prefix_keys[0]
    cache_values = prefix_values[0]
    answer_part, top_part, sum_part = attend_prefix(
        lax.all_to_all(
            outgoing.reshape(group_count * column_count, capacity, part_width),
            ("grp", "dev"),
            split_axis=0,
            concat_axis=0,
            tiled=True,
        ),
        cache_keys,
        cache_values,
    )
    answer = lax.all_to_all(answer_part, ("grp", "dev"), split_axis=0, concat_axis=0, tiled=True)
    far_top = lax.all_to_all(top_part, ("grp", "dev"), split_axis=0, concat_axis=0, tiled=True)
    far_sum = lax.all_to_all(sum_part, ("grp", "dev"), split_axis=0, concat_axis=0, tiled=True)
    answer = answer.reshape(group_count, column_count, capacity, part_width)
    far_top = far_top.reshape(group_count, column_count, capacity, local_heads)
    far_sum = far_sum.reshape(group_count, column_count, capacity, local_heads)
    placed_answer = jnp.zeros((slot_count + capacity, model_width), jnp.bfloat16)
    placed_top = jnp.zeros((slot_count + capacity, head_count), jnp.bfloat16)
    placed_sum = jnp.zeros((slot_count + capacity, head_count), jnp.bfloat16)
    for request in range(request_total):
        own_answer = (
            lax.dynamic_index_in_dim(answer, groups[request], 0, keepdims=False)
            .transpose(1, 0, 2)
            .reshape(capacity, model_width)
        )
        own_top_rows = (
            lax.dynamic_index_in_dim(far_top, groups[request], 0, keepdims=False)
            .transpose(1, 0, 2)
            .reshape(capacity, head_count)
        )
        own_sum_rows = (
            lax.dynamic_index_in_dim(far_sum, groups[request], 0, keepdims=False)
            .transpose(1, 0, 2)
            .reshape(capacity, head_count)
        )
        placed_answer = lax.dynamic_update_slice(
            placed_answer, own_answer, (starts[request], anchor)
        )
        placed_top = lax.dynamic_update_slice(placed_top, own_top_rows, (starts[request], anchor))
        placed_sum = lax.dynamic_update_slice(placed_sum, own_sum_rows, (starts[request], anchor))
    own_top, own_sum, own_mixed = attend_suffix(
        suffix_queries, suffix_keys, suffix_values, segment, head_count
    )
    far_rows = placed_answer[:slot_count].reshape(slot_count, head_count, HD)
    context = merge_parts(
        far_rows, placed_top[:slot_count], placed_sum[:slot_count], own_top, own_sum, own_mixed
    )
    hidden_state = layer_norm(
        layer_input.astype(jnp.float32) + context.reshape(slot_count, model_width),
        attn_gain,
        attn_shift,
    ).astype(jnp.bfloat16)
    up_slice, bias_slice, down_slice = (
        lax.all_gather(up_weight, "grp", axis=1, tiled=True),
        lax.all_gather(up_bias, "grp", axis=0, tiled=True),
        lax.all_gather(down_weight, "grp", axis=0, tiled=True),
    )
    activation = expand_rows(
        lax.all_gather(hidden_state, "dev", axis=0, tiled=True), up_slice, bias_slice
    )
    mlp_sum = lax.psum_scatter(
        jnp.dot(activation, down_slice, preferred_element_type=jnp.float32).astype(jnp.bfloat16),
        "dev",
        scatter_dimension=0,
        tiled=True,
    ).astype(jnp.float32)
    return layer_norm(
        hidden_state.astype(jnp.float32) + mlp_sum + down_bias, out_gain, out_shift
    ).astype(jnp.bfloat16)


def solution(mesh):
    placed = (
        P(("grp", "dev"), None),
        P(("grp", "dev"), None),
        P(("grp", "dev"), None),
        P(("grp", "dev"), None),
        P(("grp", "dev"), None),
        P(("grp", "dev"), None),
        P("grp", None, "dev"),
        P("grp", None, "dev"),
        P(None, ("grp", "dev")),
        P(("grp", "dev")),
        P(("grp", "dev"), None),
        P(),
        P(),
        P(),
        P(),
        P(),
    )
    return jax.shard_map(
        on_device, mesh=mesh, in_specs=placed, out_specs=P(("grp", "dev"), None), check_vma=False
    )
```

profile of v0, /device:TPU:0, one launch (start us, length us, event | category | flops | bytes accessed | tf_op | source)
XLA Modules:
  0.0 412.4 jit_solution(14731411691771604662)
XLA Ops:
  57.2 11.2 %all-to-all-start = ((bf16[128,32,128]{2,1,0:T(8,128)(2,1)}), bf16[128,32,128]{2,1,0:T(8,128)(2,1)S(1)}, u32[]{:S(2)}, u32[]{:S(2)}) async-start(bf16[128,32,128]{2,1,0:T(8,128)(2,1)} %bitcast.51), calls=%async_computation | async-start | bytes 2097152 | tf_op jit(solution)/shard_map/all_to_all | solution.py:150
  69.2 18.3 %all-to-all-done = bf16[128,32,128]{2,1,0:T(8,128)(2,1)S(1)} async-done(((bf16[128,32,128]{2,1,0:T(8,128)(2,1)}), bf16[128,32,128]{2,1,0:T(8,128)(2,1)S(1)}, u32[]{:S(2)}, u32[]{:S(2)}) %all-to-all-start) | async-done | bytes 1048608 | tf_op jit(solution)/shard_map/all_to_all | solution.py:150
  87.5 41.1 %while.14 = (s32[]{:T(128)}, bf16[8,512,128]{2,1,0:T(8,128)(2,1)}, bf16[8,512,1]{1,0,2:T(8,128)(2,1)S(1)}, bf16[8,512,1]{1,0,2:T(8,128)(2,1)S(1)}, bf16[8,512,1,...) while((s32[]{:T(128)}, bf16[8,512,128]{2,1,0:T(8,128)(2,1)}, ...), condition=%wide.region_4.5_spmd, body=%wide.region_1.4_spmd.sunk | while | flops 1090650112 | bytes 31745168 | solution.py:61
  126.3 2.2 fusion.119
  129.3 4.6 %all-to-all-start.2 = ((bf16[128,32,1]{1,2,0:T(2,128)(2,1)}), bf16[128,32,1]{1,2,0:T(2,128)(2,1)S(1)}, u32[]{:S(2)}, u32[]{:S(2)}) async-start(bf16[128,32,1]{1,2,0:T(2,128)(2,1)} %reshape.401), calls=%async_computation.2 | async-start | bytes 131072 | tf_op jit(solution)/shard_map/all_to_all | solution.py:162
  134.6 8.8 %all-to-all-done.2 = bf16[128,32,1]{1,2,0:T(2,128)(2,1)S(1)} async-done(((bf16[128,32,1]{1,2,0:T(2,128)(2,1)}), bf16[128,32,1]{1,2,0:T(2,128)(2,1)S(1)}, u32[]{:S(2)}, u32[]{:S(2)}) %all-to-all-start.2) | async-done | bytes 8224 | tf_op jit(solution)/shard_map/all_to_all | solution.py:162
  143.4 4.6 %all-to-all-start.1 = ((bf16[128,32,1]{1,2,0:T(2,128)(2,1)}), bf16[128,32,1]{1,2,0:T(2,128)(2,1)S(1)}, u32[]{:S(2)}, u32[]{:S(2)}) async-start(bf16[128,32,1]{1,2,0:T(2,128)(2,1)} %reshape.400), calls=%async_computation.1 | async-start | bytes 131072 | tf_op jit(solution)/shard_map/all_to_all | solution.py:161
  148.0 9.4 %all-to-all-done.1 = bf16[128,32,1]{1,2,0:T(2,128)(2,1)S(1)} async-done(((bf16[128,32,1]{1,2,0:T(2,128)(2,1)}), bf16[128,32,1]{1,2,0:T(2,128)(2,1)S(1)}, u32[]{:S(2)}, u32[]{:S(2)}) %all-to-all-start.1) | async-done | bytes 8224 | tf_op jit(solution)/shard_map/all_to_all | solution.py:161
  157.4 4.6 %all-to-all-start.3 = ((bf16[128,32,128]{2,1,0:T(8,128)(2,1)}), bf16[128,32,128]{2,1,0:T(8,128)(2,1)S(1)}, u32[]{:S(2)}, u32[]{:S(2)}) async-start(bf16[128,32,128]{2,1,0:T(8,128)(2,1)} %bitcast.380), calls=%async_computation.3 | async-start | bytes 2097152 | tf_op jit(solution)/shard_map/all_to_all | solution.py:160
  170.3 10.7 %all-to-all-done.3 = bf16[128,32,128]{2,1,0:T(8,128)(2,1)S(1)} async-done(((bf16[128,32,128]{2,1,0:T(8,128)(2,1)}), bf16[128,32,128]{2,1,0:T(8,128)(2,1)S(1)}, u32[]{:S(2)}, u32[]{:S(2)}) %all-to-all-start.3) | async-done | bytes 1048608 | tf_op jit(solution)/shard_map/all_to_all | solution.py:160
  187.3 4.9 %dynamic_update_slice.131 = bf16[160,2048]{0,1:T(8,128)(2,1)S(1)} dynamic-update-slice(bf16[160,2048]{0,1:T(8,128)(2,1)S(1)} %broadcast_in_dim.168, bf16[32,2048]{0,1:T(8,128)(2,1)} %bitcast.379, s32[]{:T(128)S(6)} %select_n.134, s32[]{:T(128)} %constant.96.clone.1) | dynamic-update-slice | bytes 262148 | tf_op jit(solution)/shard_map/dynamic_update_slice | solution.py:185
  192.2 5.9 %dynamic_update_slice.132 = bf16[160,2048]{0,1:T(8,128)(2,1)S(1)} dynamic-update-slice(bf16[160,2048]{0,1:T(8,128)(2,1)S(1)} %dynamic_update_slice.131, bf16[32,2048]{0,1:T(8,128)(2,1)} %bitcast.378, s32[]{:T(128)S(6)} %select_n.137, s32[]{:T(128)} %constant.96.clone.1) | dynamic-update-slice | bytes 262148 | tf_op jit(solution)/shard_map/dynamic_update_slice | solution.py:185
  198.1 5.9 %dynamic_update_slice.133 = bf16[160,2048]{0,1:T(8,128)(2,1)S(1)} dynamic-update-slice(bf16[160,2048]{0,1:T(8,128)(2,1)S(1)} %dynamic_update_slice.132, bf16[32,2048]{0,1:T(8,128)(2,1)} %bitcast.377, s32[]{:T(128)S(6)} %select_n.140, s32[]{:T(128)} %constant.96.clone.1) | dynamic-update-slice | bytes 262148 | tf_op jit(solution)/shard_map/dynamic_update_slice | solution.py:185
  204.1 5.9 %dynamic_update_slice.134 = bf16[160,2048]{0,1:T(8,128)(2,1)S(1)} dynamic-update-slice(bf16[160,2048]{0,1:T(8,128)(2,1)S(1)} %dynamic_update_slice.133, bf16[32,2048]{0,1:T(8,128)(2,1)} %bitcast.376, s32[]{:T(128)S(6)} %select_n.143, s32[]{:T(128)} %constant.96.clone.1) | dynamic-update-slice | bytes 262148 | tf_op jit(solution)/shard_map/dynamic_update_slice | solution.py:185
  210.0 5.9 %dynamic_update_slice.135 = bf16[160,2048]{0,1:T(8,128)(2,1)S(1)} dynamic-update-slice(bf16[160,2048]{0,1:T(8,128)(2,1)S(1)} %dynamic_update_slice.134, bf16[32,2048]{0,1:T(8,128)(2,1)} %bitcast.375, s32[]{:T(128)S(6)} %select_n.146, s32[]{:T(128)} %constant.96.clone.1) | dynamic-update-slice | bytes 262148 | tf_op jit(solution)/shard_map/dynamic_update_slice | solution.py:185
  216.0 4.0 dynamic_update_slice.136
  220.0 4.0 dynamic_update_slice.137
  224.0 4.2 %dynamic_update_slice.138 = bf16[160,2048]{0,1:T(8,128)(2,1)S(1)} dynamic-update-slice(bf16[160,2048]{0,1:T(8,128)(2,1)S(1)} %dynamic_update_slice.137, bf16[32,2048]{0,1:T(8,128)(2,1)S(1)} %bitcast.372, s32[]{:T(128)S(6)} %select_n.155, s32[]{:T(128)} %constant.96.clone.1) | dynamic-update-slice | bytes 262148 | tf_op jit(solution)/shard_map/dynamic_update_slice | solution.py:185
  228.3 2.8 fusion.36
  235.9 12.8 %all-reduce.1 = bf16[512]{0:T(512)(128)(2,1)S(1)} all-reduce(bf16[512]{0:T(512)(128)(2,1)S(1)} %dynamic-update-slice), channel_id=1, replica_groups=mesh['grp'=8,'dev'=16] {'grp'}, use_global_device_ids=true, to_apply=%add.1 | all-reduce | flops 512 | bytes 2048
  248.8 52.0 %all-gather.4.cloned.1.call-done = bf16[2048,2048]{1,0:T(8,128)(2,1)} async-done(((bf16[128,2048]{1,0:T(8,128)(2,1)}), bf16[2048,2048]{1,0:T(8,128)(2,1)}) %all-gather.4.cloned.1.call-update) | async-done | bytes 8388624 | tf_op jit(solution)/shard_map/all_gather | solution.py:208
  300.8 15.2 %convolution_convert_fusion = bf16[2048,2048]{1,0:T(8,128)(2,1)} fusion(bf16[512,2048]{1,0:T(8,128)(2,1)} %all-gather.8.cloned.1.call-done, bf16[2048,2048]{1,0:T(8,128)(2,1)} %all-gather.4.cloned.1.call-done, bf16[2048,512]{0,1:T(8,128)(2,1)} %all-gather.6.cloned.1.call-done, f32[512]{0:T(512)S(1)} %convert_element_type.97), kind=kOutput, calls=%fused_computation.17 | convolution fusion | flops 8604614656 | bytes 20973568 | tf_op jit(solution)/shard_map/dot_general | solution.py:211
  316.1 84.9 %reduce-scatter.2.cloned.1.call-done = bf16[128,2048]{1,0:T(8,128)(2,1)} async-done(((bf16[2048,2048]{1,0:T(8,128)(2,1)}), bf16[128,2048]{1,0:T(8,128)(2,1)}) %reduce-scatter.2.cloned.1.call-update) | async-done | bytes 524304 | tf_op jit(solution)/shard_map/reduce_scatter | solution.py:210
  403.7 2.2 add_convert_fusion
  (215 shorter events, 82.7 us)
Async XLA Ops:
  6.5 157.7 %copy-start = (bf16[128,2048]{1,0:T(8,128)(2,1)S(1)}, bf16[128,2048]{1,0:T(8,128)(2,1)}, u32[]{:S(2)}) copy-start(bf16[128,2048]{1,0:T(8,128)(2,1)} %param.19) | copy-start | bytes 1572868
  6.5 80.9 %copy-start.1 = (bf16[1,4096,128]{2,1,0:T(8,128)(2,1)S(1)}, bf16[1,4096,128]{2,1,0:T(8,128)(2,1)}, u32[]{:S(2)}) copy-start(bf16[1,4096,128]{2,1,0:T(8,128)(2,1)} %param.24) | copy-start | bytes 3145732
  6.5 242.2 %all-gather.6.cloned.1.call-start = ((), (), s32[]{:S(2)}) async-start(), calls=%async_computation.6 | async-start | bytes 2359296 | tf_op jit(solution)/shard_map/all_gather | solution.py:203
  57.2 30.3 %all-to-all-start = ((bf16[128,32,128]{2,1,0:T(8,128)(2,1)}), bf16[128,32,128]{2,1,0:T(8,128)(2,1)S(1)}, u32[]{:S(2)}, u32[]{:S(2)}) async-start(bf16[128,32,128]{2,1,0:T(8,128)(2,1)} %bitcast.51), calls=%async_computation | async-start | bytes 2097152 | tf_op jit(solution)/shard_map/all_to_all | solution.py:150
  68.4 180.4 %all-gather.8.cloned.1.call-start = ((), (), s32[]{:S(2)}) async-start(), calls=%async_computation.7 | async-start | bytes 2359296 | tf_op jit(solution)/shard_map/all_gather | solution.py:205
  87.5 60.5 %copy-start.7 = (s32[1,8]{1,0:T(1,128)S(1)}, s32[1,8]{1,0:T(1,128)}, u32[]{:S(2)}) copy-start(s32[1,8]{1,0:T(1,128)} %param.22) | copy-start | bytes 100
  87.5 76.8 %copy-start.4 = (bf16[128,2048]{1,0:T(8,128)(2,1)S(1)}, bf16[128,2048]{1,0:T(8,128)(2,1)}, u32[]{:S(2)}) copy-start(bf16[128,2048]{1,0:T(8,128)(2,1)} %param.18) | copy-start | bytes 1572868
  94.0 1.5 copy-start.12
  99.1 1.5 copy-start.12
  104.3 1.5 copy-start.12
  129.3 14.0 %all-to-all-start.2 = ((bf16[128,32,1]{1,2,0:T(2,128)(2,1)}), bf16[128,32,1]{1,2,0:T(2,128)(2,1)S(1)}, u32[]{:S(2)}, u32[]{:S(2)}) async-start(bf16[128,32,1]{1,2,0:T(2,128)(2,1)} %reshape.401), calls=%async_computation.2 | async-start | bytes 131072 | tf_op jit(solution)/shard_map/all_to_all | solution.py:162
  143.4 14.0 %all-to-all-start.1 = ((bf16[128,32,1]{1,2,0:T(2,128)(2,1)}), bf16[128,32,1]{1,2,0:T(2,128)(2,1)S(1)}, u32[]{:S(2)}, u32[]{:S(2)}) async-start(bf16[128,32,1]{1,2,0:T(2,128)(2,1)} %reshape.400), calls=%async_computation.1 | async-start | bytes 131072 | tf_op jit(solution)/shard_map/all_to_all | solution.py:161
  157.4 23.7 %all-to-all-start.3 = ((bf16[128,32,128]{2,1,0:T(8,128)(2,1)}), bf16[128,32,128]{2,1,0:T(8,128)(2,1)S(1)}, u32[]{:S(2)}, u32[]{:S(2)}) async-start(bf16[128,32,128]{2,1,0:T(8,128)(2,1)} %bitcast.380), calls=%async_computation.3 | async-start | bytes 2097152 | tf_op jit(solution)/shard_map/all_to_all | solution.py:160
  162.0 138.8 %all-gather.4.cloned.1.call-start = ((), (), s32[]{:S(2)}) async-start(), calls=%async_computation.5 | async-start | bytes 8912896 | tf_op jit(solution)/shard_map/all_gather | solution.py:208
  228.3 4.4 %copy-start.3 = (bf16[128,2048]{1,0:T(8,128)(2,1)S(1)}, bf16[128,2048]{1,0:T(8,128)(2,1)}, u32[]{:S(2)}) copy-start(bf16[128,2048]{1,0:T(8,128)(2,1)} %param.21) | copy-start | bytes 1572868
  228.3 4.9 %copy-start.8 = (f32[2048]{0:T(1024)S(1)}, f32[2048]{0:T(1024)}, u32[]{:S(2)}) copy-start(f32[2048]{0:T(1024)} %param.31) | copy-start | bytes 24580
  228.3 4.9 %copy-start.9 = (f32[2048]{0:T(1024)S(1)}, f32[2048]{0:T(1024)}, u32[]{:S(2)}) copy-start(f32[2048]{0:T(1024)} %param.30) | copy-start | bytes 24580
  231.1 3.3 copy-start.14
  231.1 4.5 %copy-start.13 = (bf16[64]{0:T(256)(128)(2,1)S(1)}, bf16[64]{0:T(256)(128)(2,1)}, u32[]{:S(2)}) copy-start(bf16[64]{0:T(256)(128)(2,1)} %param.27) | copy-start | bytes 388
  234.3 166.6 %reduce-scatter.2.cloned.1.call-start = ((), (), s32[]{:S(2)}) async-start(), calls=%async_computation.8 | async-start | bytes 8912896 | tf_op jit(solution)/shard_map/reduce_scatter | solution.py:210
  316.0 84.9 %copy-start.2 = (bf16[128,2048]{1,0:T(8,128)(2,1)S(1)}, bf16[128,2048]{1,0:T(8,128)(2,1)}, u32[]{:S(2)}) copy-start(bf16[128,2048]{1,0:T(8,128)(2,1)} %add_convert_fusion.1) | copy-start | bytes 1572868
  316.0 84.9 %copy-start.6 = (f32[2048]{0:T(1024)S(1)}, f32[2048]{0:T(1024)}, u32[]{:S(2)}) copy-start(f32[2048]{0:T(1024)} %param.29) | copy-start | bytes 24580
  316.0 87.6 %copy-start.10 = (f32[2048]{0:T(1024)S(1)}, f32[2048]{0:T(1024)}, u32[]{:S(2)}) copy-start(f32[2048]{0:T(1024)} %param.33) | copy-start | bytes 24580
  316.0 87.6 %copy-start.11 = (f32[2048]{0:T(1024)S(1)}, f32[2048]{0:T(1024)}, u32[]{:S(2)}) copy-start(f32[2048]{0:T(1024)} %param.32) | copy-start | bytes 24580
  (6 other events, 8.6 us)
Sparse Core Ops, SparseCore 0:
  9.1 27.6 all-gather.5
  71.0 26.2 all-gather.7
  234.5 66.3 all-gather.3
  316.2 84.7 reduce-scatter.1
where the time goes:
time: 414 us; the launch traced here: 412 us
  waiting for transfers between devices  186 us (45%)
  local copies, waits for them, and re-layouts  69.7 us (17%)
  matrix products  46.3 us (11%)
  between operations  44.2 us (11%)
  other arithmetic  28.4 us (7%)
  starting transfers between devices  25.1 us (6%)
  blocking collectives  12.8 us (3%)
    reduce_scatter x1, waiting for transfers between devices, on_device(): lax.psum_scatter(jnp.dot(activation, down_slice, preferred_element_type=j...  84.9 us
    all_gather x1, waiting for transfers between devices, on_device(): lax.all_gather(hidden_state, 'dev', axis=0, tiled=True)  52 us
    dynamic_update_slice x8, local copies, waits for them, and re-layouts, on_device(): lax.dynamic_update_slice(placed_answer, own_answer, (starts[request], anc...  40.9 us
    all_to_all x1, waiting for transfers between devices, on_device(): lax.all_to_all(outgoing.reshape(group_count * column_count, capacity, par...  18.3 us
    dot_general x8, matrix products, one_block(): jnp.einsum('hqk,khd->qhd', weights.astype(jnp.bfloat16), value_heads, pre...  17.2 us
    dot_general x1, matrix products, on_device(): jnp.dot(activation, down_slice, preferred_element_type=jnp.float32)  15.2 us
    unnamed x1, blocking collectives  12.8 us
    reduce_sum x8, other arithmetic, one_block(): row_sum = jnp.sum(weights, axis=2)  12 us
  transfers between devices with their start and end apart: 8, of which 6 were waited for; matrix products, arithmetic and copies ran while one was open for 30% of the time, Pallas kernels for 0%

commit v1 on v0

--- a/solution.py
+++ b/solution.py
@@ -6,6 +6,28 @@
 
 HD = 128
 norm_eps = 1e-12
+
+
+def laid_out(pieces, dim):
+    pieces = jnp.moveaxis(pieces, 0, dim)
+    lengths = pieces.shape
+    return pieces.reshape(*lengths[:dim], lengths[dim] * lengths[dim + 1], *lengths[dim + 2 :])
+
+
+def gather_around(array, axis, dim):
+    size = lax.axis_size(axis)
+    pairs = [(i, (i + 1) % size) for i in range(size)]
+    back = [(b, a) for a, b in pairs]
+    lower, upper = ([], [])
+    for step in range(size - 1):
+        if step % 2 == 0:
+            lower.append(lax.ppermute(lower[-1] if lower else array, axis, pairs))
+        else:
+            upper.append(lax.ppermute(upper[-1] if upper else array, axis, back))
+    blocks = jnp.stack([*lower[::-1], array, *upper])
+    shift = lax.axis_index(axis) - len(lower)
+    blocks = blocks[(jnp.arange(size) - shift) % size]
+    return laid_out(blocks, dim)
 
 
 def layer_norm(summed, norm_gain, norm_shift):
@@ -204,9 +226,7 @@
         lax.all_gather(up_bias, "grp", axis=0, tiled=True),
         lax.all_gather(down_weight, "grp", axis=0, tiled=True),
     )
-    activation = expand_rows(
-        lax.all_gather(hidden_state, "dev", axis=0, tiled=True), up_slice, bias_slice
-    )
+    activation = expand_rows(gather_around(hidden_state, "dev", 0), up_slice, bias_slice)
     mlp_sum = lax.psum_scatter(
         jnp.dot(activation, down_slice, preferred_element_type=jnp.float32).astype(jnp.bfloat16),
         "dev",

time: 414 us -> 501 us (1.21); the launches traced: 412 us -> 492 us
  starting transfers between devices: 25.1 us -> 64.2 us
  local copies, waits for them, and re-layouts: 69.7 us -> 95.3 us
  matrix products: 46.3 us -> 55.8 us
    ppermute x0 -> x15, waiting for transfers between devices: none -> 63.8 us  [the longest x8 62.3 us: gather_around(): lower.append(lax.ppermute(lower[-1] if lower else array, axis, pairs))]
    all_gather x1 -> x0, waiting for transfers between devices: 52 us -> none  [on_device(): lax.all_gather(hidden_state, 'dev', axis=0, tiled=True)]
    ppermute x0 -> x15, starting transfers between devices: none -> 39.1 us  [the longest x7 38.1 us: gather_around(): upper.append(lax.ppermute(upper[-1] if upper else array, axis, back))]
    unnamed x33 -> x62, local copies, waits for them, and re-layouts: 1.93 us -> 23.7 us
    dot_general x8, matrix products: 10.7 us -> 21.2 us  [one_block(): jnp.einsum('qhd,khd->hqk', query_block, key_heads, preferred_element_type...]
    gather x0 -> x1, local copies, waits for them, and re-layouts: none -> 8.37 us  [gather_around(): blocks = blocks[(jnp.arange(size) - shift) % size]]
    reduce_scatter x1, waiting for transfers between devices: 84.9 us -> 78.8 us  [on_device(): lax.psum_scatter(jnp.dot(activation, down_slice, preferred_element_type=j...]
  transfers between devices with their start and end apart: 8 -> 22, of which waited for: 6 -> 14; matrix products, arithmetic and copies ran while one was open for 30% -> 8% of each run, Pallas kernels for 0% -> 0%
where the time goes in v1:
time: 501 us; the launch traced here: 492 us
  waiting for transfers between devices  191 us (38%)
  local copies, waits for them, and re-layouts  95.3 us (19%)
  starting transfers between devices  64.2 us (13%)
  matrix products  55.8 us (11%)
  between operations  44.4 us (9%)
  other arithmetic  27.5 us (5%)
  blocking collectives  12.8 us (3%)
    reduce_scatter x1, waiting for transfers between devices, on_device(): lax.psum_scatter(jnp.dot(activation, down_slice, preferred_element_type=j...  78.8 us
    ppermute x8, waiting for transfers between devices, gather_around(): lower.append(lax.ppermute(lower[-1] if lower else array, axis, pairs))  62.3 us
    dynamic_update_slice x8, local copies, waits for them, and re-layouts, on_device(): lax.dynamic_update_slice(placed_answer, own_answer, (starts[request], anc...  38.7 us
    ppermute x7, starting transfers between devices, gather_around(): upper.append(lax.ppermute(upper[-1] if upper else array, axis, back))  38.1 us
    unnamed x62, local copies, waits for them, and re-layouts  23.7 us
    dot_general x8, matrix products, one_block(): jnp.einsum('qhd,khd->hqk', query_block, key_heads, preferred_element_type...  21.2 us
    all_to_all x1, waiting for transfers between devices, on_device(): lax.all_to_all(outgoing.reshape(group_count * column_count, capacity, par...  19 us
    dot_general x8, matrix products, one_block(): jnp.einsum('hqk,khd->qhd', weights.astype(jnp.bfloat16), value_heads, pre...  17.1 us
  transfers between devices with their start and end apart: 22, of which 14 were waited for; matrix products, arithmetic and copies ran while one was open for 8% of the time, Pallas kernels for 0%

profile of v1, /device:TPU:0, one launch (start us, length us, event | category | flops | bytes accessed | tf_op | source)
XLA Modules:
  0.0 492.0 jit_solution(6635212174220183825)
XLA Ops:
  56.2 11.2 %all-to-all-start = ((bf16[128,32,128]{2,1,0:T(8,128)(2,1)}), bf16[128,32,128]{2,1,0:T(8,128)(2,1)S(1)}, u32[]{:S(2)}, u32[]{:S(2)}) async-start(bf16[128,32,128]{2,1,0:T(8,128)(2,1)} %bitcast.51), calls=%async_computation | async-start | bytes 2097152 | tf_op jit(solution)/shard_map/all_to_all | solution.py:172
  67.5 19.0 %all-to-all-done = bf16[128,32,128]{2,1,0:T(8,128)(2,1)S(1)} async-done(((bf16[128,32,128]{2,1,0:T(8,128)(2,1)}), bf16[128,32,128]{2,1,0:T(8,128)(2,1)S(1)}, u32[]{:S(2)}, u32[]{:S(2)}) %all-to-all-start) | async-done | bytes 1048608 | tf_op jit(solution)/shard_map/all_to_all | solution.py:172
  86.5 51.6 %while.14 = (s32[]{:T(128)}, bf16[8,512,128]{2,1,0:T(8,128)(2,1)}, bf16[8,512,1]{1,0,2:T(8,128)(2,1)S(1)}, bf16[8,512,1]{1,0,2:T(8,128)(2,1)S(1)}, bf16[8,512,1,...) while((s32[]{:T(128)}, bf16[8,512,128]{2,1,0:T(8,128)(2,1)}, ...), condition=%wide.region_4.5_spmd, body=%wide.region_1.4_spmd.sunk | while | flops 1090650112 | bytes 31745668 | solution.py:83
  144.2 8.7 %all-to-all-done.1 = bf16[128,32,1]{1,2,0:T(2,128)(2,1)S(1)} async-done(((bf16[128,32,1]{1,2,0:T(2,128)(2,1)}), bf16[128,32,1]{1,2,0:T(2,128)(2,1)S(1)}, u32[]{:S(2)}, u32[]{:S(2)}) %all-to-all-start.1) | async-done | bytes 8224 | tf_op jit(solution)/shard_map/all_to_all | solution.py:183
  157.5 9.5 %all-to-all-done.2 = bf16[128,32,1]{1,2,0:T(2,128)(2,1)S(1)} async-done(((bf16[128,32,1]{1,2,0:T(2,128)(2,1)}), bf16[128,32,1]{1,2,0:T(2,128)(2,1)S(1)}, u32[]{:S(2)}, u32[]{:S(2)}) %all-to-all-start.2) | async-done | bytes 8224 | tf_op jit(solution)/shard_map/all_to_all | solution.py:184
  179.0 11.7 %all-to-all-done.3 = bf16[128,32,128]{2,1,0:T(8,128)(2,1)S(1)} async-done(((bf16[128,32,128]{2,1,0:T(8,128)(2,1)}), bf16[128,32,128]{2,1,0:T(8,128)(2,1)S(1)}, u32[]{:S(2)}, u32[]{:S(2)}) %all-to-all-start.3) | async-done | bytes 1048608 | tf_op jit(solution)/shard_map/all_to_all | solution.py:182
  198.5 6.0 %dynamic_update_slice.132 = bf16[160,2048]{0,1:T(8,128)(2,1)S(1)} dynamic-update-slice(bf16[160,2048]{0,1:T(8,128)(2,1)S(1)} %dynamic_update_slice.131, bf16[32,2048]{0,1:T(8,128)(2,1)} %bitcast.414, s32[]{:T(128)S(6)} %select_n.161, s32[]{:T(128)} %constant.114.clone.1) | dynamic-update-slice | bytes 262148 | tf_op jit(solution)/shard_map/dynamic_update_slice | solution.py:207
  204.4 5.9 %dynamic_update_slice.133 = bf16[160,2048]{0,1:T(8,128)(2,1)S(1)} dynamic-update-slice(bf16[160,2048]{0,1:T(8,128)(2,1)S(1)} %dynamic_update_slice.132, bf16[32,2048]{0,1:T(8,128)(2,1)} %bitcast.413, s32[]{:T(128)S(6)} %select_n.164, s32[]{:T(128)} %constant.114.clone.1) | dynamic-update-slice | bytes 262148 | tf_op jit(solution)/shard_map/dynamic_update_slice | solution.py:207
  210.4 5.9 %dynamic_update_slice.134 = bf16[160,2048]{0,1:T(8,128)(2,1)S(1)} dynamic-update-slice(bf16[160,2048]{0,1:T(8,128)(2,1)S(1)} %dynamic_update_slice.133, bf16[32,2048]{0,1:T(8,128)(2,1)} %bitcast.412, s32[]{:T(128)S(6)} %select_n.167, s32[]{:T(128)} %constant.114.clone.1) | dynamic-update-slice | bytes 262148 | tf_op jit(solution)/shard_map/dynamic_update_slice | solution.py:207
  216.4 5.9 %dynamic_update_slice.135 = bf16[160,2048]{0,1:T(8,128)(2,1)S(1)} dynamic-update-slice(bf16[160,2048]{0,1:T(8,128)(2,1)S(1)} %dynamic_update_slice.134, bf16[32,2048]{0,1:T(8,128)(2,1)} %bitcast.411, s32[]{:T(128)S(6)} %select_n.170, s32[]{:T(128)} %constant.114.clone.1) | dynamic-update-slice | bytes 262148 | tf_op jit(solution)/shard_map/dynamic_update_slice | solution.py:207
  238.9 15.2 %collective-permute-done = bf16[128,2048]{1,0:T(8,128)(2,1)S(1)} collective-permute-done((bf16[128,2048]{1,0:T(8,128)(2,1)S(1)}, bf16[128,2048]{1,0:T(8,128)(2,1)S(1)}, u32[]{:S(2)}, u32[]{:S(2)}) %collective-permute-start) | collective-permute-done | bytes 524320 | tf_op jit(solution)/shard_map/ppermute | solution.py:24
  259.4 9.9 %collective-permute-done.1 = bf16[128,2048]{1,0:T(8,128)(2,1)S(1)} collective-permute-done((bf16[128,2048]{1,0:T(8,128)(2,1)S(1)}, bf16[128,2048]{1,0:T(8,128)(2,1)S(1)}, u32[]{:S(2)}, u32[]{:S(2)}) %collective-permute-start.1) | collective-permute-done | bytes 524320 | tf_op jit(solution)/shard_map/ppermute | solution.py:24
  274.7 9.0 %collective-permute-done.2 = bf16[128,2048]{1,0:T(8,128)(2,1)S(1)} collective-permute-done((bf16[128,2048]{1,0:T(8,128)(2,1)S(1)}, bf16[128,2048]{1,0:T(8,128)(2,1)S(1)}, u32[]{:S(2)}, u32[]{:S(2)}) %collective-permute-start.2) | collective-permute-done | bytes 524320 | tf_op jit(solution)/shard_map/ppermute | solution.py:24
  283.6 5.3 %collective-permute-start.10 = (bf16[128,2048]{1,0:T(8,128)(2,1)S(1)}, bf16[128,2048]{1,0:T(8,128)(2,1)S(1)}, u32[]{:S(2)}, u32[]{:S(2)}) collective-permute-start(bf16[128,2048]{1,0:T(8,128)(2,1)S(1)} %collective-permute-done.9), channel_id=1, source_target_pairs={{1,0},{2,1},{3,2},{4,3},{5,4},{6,5},{7,6},{8,7},{9,8},{10,9},{11,1... | collective-permute-start | bytes 1572872 | tf_op jit(solution)/shard_map/ppermute | solution.py:26
  289.0 8.1 %collective-permute-done.3 = bf16[128,2048]{1,0:T(8,128)(2,1)S(1)} collective-permute-done((bf16[128,2048]{1,0:T(8,128)(2,1)S(1)}, bf16[128,2048]{1,0:T(8,128)(2,1)S(1)}, u32[]{:S(2)}, u32[]{:S(2)}) %collective-permute-start.3) | collective-permute-done | bytes 524320 | tf_op jit(solution)/shard_map/ppermute | solution.py:24
  303.2 6.4 %collective-permute-done.4 = bf16[128,2048]{1,0:T(8,128)(2,1)S(1)} collective-permute-done((bf16[128,2048]{1,0:T(8,128)(2,1)S(1)}, bf16[128,2048]{1,0:T(8,128)(2,1)S(1)}, u32[]{:S(2)}, u32[]{:S(2)}) %collective-permute-start.4) | collective-permute-done | bytes 524320 | tf_op jit(solution)/shard_map/ppermute | solution.py:24
  310.7 5.8 %collective-permute-start.12 = (bf16[128,2048]{1,0:T(8,128)(2,1)S(1)}, bf16[128,2048]{1,0:T(8,128)(2,1)}, u32[]{:S(2)}, u32[]{:S(2)}) collective-permute-start(bf16[128,2048]{1,0:T(8,128)(2,1)S(1)} %collective-permute-done.11), channel_id=1, source_target_pairs={{1,0},{2,1},{3,2},{4,3},{5,4},{6,5},{7,6},{8,7},{9,8},{10,9},{11,1... | collective-permute-start | bytes 1572872 | tf_op jit(solution)/shard_map/ppermute | solution.py:26
  316.5 6.5 %collective-permute-done.5 = bf16[128,2048]{1,0:T(8,128)(2,1)S(1)} collective-permute-done((bf16[128,2048]{1,0:T(8,128)(2,1)S(1)}, bf16[128,2048]{1,0:T(8,128)(2,1)S(1)}, u32[]{:S(2)}, u32[]{:S(2)}) %collective-permute-start.5) | collective-permute-done | bytes 524320 | tf_op jit(solution)/shard_map/ppermute | solution.py:24
  324.1 5.9 %collective-permute-start.13 = (bf16[128,2048]{1,0:T(8,128)(2,1)}, bf16[128,2048]{1,0:T(8,128)(2,1)}, u32[]{:S(2)}, u32[]{:S(2)}) collective-permute-start(bf16[128,2048]{1,0:T(8,128)(2,1)} %collective-permute-done.12), channel_id=1, source_target_pairs={{1,0},{2,1},{3,2},{4,3},{5,4},{6,5},{7,6},{8,7},{9,8},{10,9},{11,1... | collective-permute-start | bytes 1572872 | tf_op jit(solution)/shard_map/ppermute | solution.py:26
  330.0 7.3 %collective-permute-done.6 = bf16[128,2048]{1,0:T(8,128)(2,1)} collective-permute-done((bf16[128,2048]{1,0:T(8,128)(2,1)S(1)}, bf16[128,2048]{1,0:T(8,128)(2,1)}, u32[]{:S(2)}, u32[]{:S(2)}) %collective-permute-start.6) | collective-permute-done | bytes 524320 | tf_op jit(solution)/shard_map/ppermute | solution.py:24
  339.1 12.8 %all-reduce.1 = bf16[512]{0:T(512)(128)(2,1)S(1)} all-reduce(bf16[512]{0:T(512)(128)(2,1)S(1)} %dynamic-update-slice), channel_id=1, replica_groups=mesh['grp'=8,'dev'=16] {'grp'}, use_global_device_ids=true, to_apply=%add.1 | all-reduce | flops 512 | bytes 2048
  377.9 8.4 %gather_fusion = bf16[16,128,2048]{2,1,0:T(8,128)(2,1)} fusion(bf16[16,128,2048]{2,1,0:T(8,128)(2,1)} %bitcast_dynamic-update-slice_fusion, s32[1024]{0:T(1024)S(1)} %pad_clamp_fusion), kind=kCustom, calls=%fused_computation | custom fusion | bytes 16777280 | tf_op jit(solution)/shard_map/gather | solution.py:29
  386.3 15.3 %convolution_convert_fusion = bf16[2048,2048]{1,0:T(8,128)(2,1)} fusion(bf16[512,2048]{1,0:T(8,128)(2,1)} %all-gather.5.cloned.1.call-done, bf16[2048,2048]{1,0:T(8,128)(2,1)} %bitcast.405, bf16[2048,512]{0,1:T(8,128)(2,1)} %all-gather.3.cloned.1.call-done, f32[512]{0:T(512)S(1)} %convert_element_type.97), kind=kOutput, calls=%fused_computation.18 | convolution fusion | flops 8604614656 | bytes 20973568 | tf_op jit(solution)/shard_map/dot_general | solution.py:231
  401.6 78.8 %reduce-scatter.2.cloned.1.call-done = bf16[128,2048]{1,0:T(8,128)(2,1)} async-done(((bf16[2048,2048]{1,0:T(8,128)(2,1)}), bf16[128,2048]{1,0:T(8,128)(2,1)}) %reduce-scatter.2.cloned.1.call-update) | async-done | bytes 524304 | tf_op jit(solution)/shard_map/reduce_scatter | solution.py:230
  (275 shorter events, 168.7 us)
Async XLA Ops:
  6.5 166.3 %copy-start = (bf16[128,2048]{1,0:T(8,128)(2,1)S(1)}, bf16[128,2048]{1,0:T(8,128)(2,1)}, u32[]{:S(2)}) copy-start(bf16[128,2048]{1,0:T(8,128)(2,1)} %param.19) | copy-start | bytes 1572868
  56.2 30.3 %all-to-all-start = ((bf16[128,32,128]{2,1,0:T(8,128)(2,1)}), bf16[128,32,128]{2,1,0:T(8,128)(2,1)S(1)}, u32[]{:S(2)}, u32[]{:S(2)}) async-start(bf16[128,32,128]{2,1,0:T(8,128)(2,1)} %bitcast.51), calls=%async_computation | async-start | bytes 2097152 | tf_op jit(solution)/shard_map/all_to_all | solution.py:172
  138.9 14.0 %all-to-all-start.1 = ((bf16[128,32,1]{1,2,0:T(2,128)(2,1)}), bf16[128,32,1]{1,2,0:T(2,128)(2,1)S(1)}, u32[]{:S(2)}, u32[]{:S(2)}) async-start(bf16[128,32,1]{1,2,0:T(2,128)(2,1)} %reshape.461), calls=%async_computation.1 | async-start | bytes 131072 | tf_op jit(solution)/shard_map/all_to_all | solution.py:183
  152.9 14.1 %all-to-all-start.2 = ((bf16[128,32,1]{1,2,0:T(2,128)(2,1)}), bf16[128,32,1]{1,2,0:T(2,128)(2,1)S(1)}, u32[]{:S(2)}, u32[]{:S(2)}) async-start(bf16[128,32,1]{1,2,0:T(2,128)(2,1)} %reshape.462), calls=%async_computation.2 | async-start | bytes 131072 | tf_op jit(solution)/shard_map/all_to_all | solution.py:184
  167.0 23.7 %all-to-all-start.3 = ((bf16[128,32,128]{2,1,0:T(8,128)(2,1)}), bf16[128,32,128]{2,1,0:T(8,128)(2,1)S(1)}, u32[]{:S(2)}, u32[]{:S(2)}) async-start(bf16[128,32,128]{2,1,0:T(8,128)(2,1)} %bitcast.107), calls=%async_computation.3 | async-start | bytes 2097152 | tf_op jit(solution)/shard_map/all_to_all | solution.py:182
  171.6 214.7 %all-gather.3.cloned.1.call-start = ((), (), s32[]{:S(2)}) async-start(), calls=%async_computation.5 | async-start | bytes 2359296 | tf_op jit(solution)/shard_map/all_gather | solution.py:225
  226.4 112.5 %copy-start.20 = (bf16[64]{0:T(256)(128)(2,1)S(1)}, bf16[64]{0:T(256)(128)(2,1)}, u32[]{:S(2)}) copy-start(bf16[64]{0:T(256)(128)(2,1)} %param.27) | copy-start | bytes 388
  237.8 16.2 %collective-permute-start = (bf16[128,2048]{1,0:T(8,128)(2,1)S(1)}, bf16[128,2048]{1,0:T(8,128)(2,1)S(1)}, u32[]{:S(2)}, u32[]{:S(2)}) collective-permute-start(bf16[128,2048]{1,0:T(8,128)(2,1)S(1)} %add_convert_fusion.1), channel_id=1, source_target_pairs={{0,1},{1,2},{2,3},{3,4},{4,5},{5,6},{6,7},{7,8},{8,9},{9,10},{10,1... | collective-permute-start | bytes 1572872 | tf_op jit(solution)/shard_map/ppermute | solution.py:24
  238.8 147.4 %all-gather.5.cloned.1.call-start = ((), (), s32[]{:S(2)}) async-start(), calls=%async_computation.6 | async-start | bytes 2359296 | tf_op jit(solution)/shard_map/all_gather | solution.py:227
  254.1 15.2 %collective-permute-start.1 = (bf16[128,2048]{1,0:T(8,128)(2,1)S(1)}, bf16[128,2048]{1,0:T(8,128)(2,1)S(1)}, u32[]{:S(2)}, u32[]{:S(2)}) collective-permute-start(bf16[128,2048]{1,0:T(8,128)(2,1)S(1)} %collective-permute-done), channel_id=1, source_target_pairs={{0,1},{1,2},{2,3},{3,4},{4,5},{5,6},{6,7},{7,8},{8,9},{9,10},{10,1... | collective-permute-start | bytes 1572872 | tf_op jit(solution)/shard_map/ppermute | solution.py:24
  254.1 15.2 %collective-permute-start.8 = (bf16[128,2048]{1,0:T(8,128)(2,1)S(1)}, bf16[128,2048]{1,0:T(8,128)(2,1)S(1)}, u32[]{:S(2)}, u32[]{:S(2)}) collective-permute-start(bf16[128,2048]{1,0:T(8,128)(2,1)S(1)} %add_convert_fusion.1), channel_id=1, source_target_pairs={{1,0},{2,1},{3,2},{4,3},{5,4},{6,5},{7,6},{8,7},{9,8},{10,9},{11,1... | collective-permute-start | bytes 1572872 | tf_op jit(solution)/shard_map/ppermute | solution.py:26
  269.3 14.3 %collective-permute-start.2 = (bf16[128,2048]{1,0:T(8,128)(2,1)S(1)}, bf16[128,2048]{1,0:T(8,128)(2,1)S(1)}, u32[]{:S(2)}, u32[]{:S(2)}) collective-permute-start(bf16[128,2048]{1,0:T(8,128)(2,1)S(1)} %collective-permute-done.1), channel_id=1, source_target_pairs={{0,1},{1,2},{2,3},{3,4},{4,5},{5,6},{6,7},{7,8},{8,9},{9,10},{10,1... | collective-permute-start | bytes 1572872 | tf_op jit(solution)/shard_map/ppermute | solution.py:24
  269.3 14.3 %collective-permute-start.9 = (bf16[128,2048]{1,0:T(8,128)(2,1)S(1)}, bf16[128,2048]{1,0:T(8,128)(2,1)S(1)}, u32[]{:S(2)}, u32[]{:S(2)}) collective-permute-start(bf16[128,2048]{1,0:T(8,128)(2,1)S(1)} %collective-permute-done.8), channel_id=1, source_target_pairs={{1,0},{2,1},{3,2},{4,3},{5,4},{6,5},{7,6},{8,7},{9,8},{10,9},{11,1... | collective-permute-start | bytes 1572872 | tf_op jit(solution)/shard_map/ppermute | solution.py:26
  283.6 13.4 %collective-permute-start.3 = (bf16[128,2048]{1,0:T(8,128)(2,1)S(1)}, bf16[128,2048]{1,0:T(8,128)(2,1)S(1)}, u32[]{:S(2)}, u32[]{:S(2)}) collective-permute-start(bf16[128,2048]{1,0:T(8,128)(2,1)S(1)} %collective-permute-done.2), channel_id=1, source_target_pairs={{0,1},{1,2},{2,3},{3,4},{4,5},{5,6},{6,7},{7,8},{8,9},{9,10},{10,1... | collective-permute-start | bytes 1572872 | tf_op jit(solution)/shard_map/ppermute | solution.py:24
  283.6 13.4 %collective-permute-start.10 = (bf16[128,2048]{1,0:T(8,128)(2,1)S(1)}, bf16[128,2048]{1,0:T(8,128)(2,1)S(1)}, u32[]{:S(2)}, u32[]{:S(2)}) collective-permute-start(bf16[128,2048]{1,0:T(8,128)(2,1)S(1)} %collective-permute-done.9), channel_id=1, source_target_pairs={{1,0},{2,1},{3,2},{4,3},{5,4},{6,5},{7,6},{8,7},{9,8},{10,9},{11,1... | collective-permute-start | bytes 1572872 | tf_op jit(solution)/shard_map/ppermute | solution.py:26
  297.0 12.5 %collective-permute-start.4 = (bf16[128,2048]{1,0:T(8,128)(2,1)S(1)}, bf16[128,2048]{1,0:T(8,128)(2,1)S(1)}, u32[]{:S(2)}, u32[]{:S(2)}) collective-permute-start(bf16[128,2048]{1,0:T(8,128)(2,1)S(1)} %collective-permute-done.3), channel_id=1, source_target_pairs={{0,1},{1,2},{2,3},{3,4},{4,5},{5,6},{6,7},{7,8},{8,9},{9,10},{10,1... | collective-permute-start | bytes 1572872 | tf_op jit(solution)/shard_map/ppermute | solution.py:24
  297.9 12.0 %collective-permute-start.11 = (bf16[128,2048]{1,0:T(8,128)(2,1)S(1)}, bf16[128,2048]{1,0:T(8,128)(2,1)S(1)}, u32[]{:S(2)}, u32[]{:S(2)}) collective-permute-start(bf16[128,2048]{1,0:T(8,128)(2,1)S(1)} %collective-permute-done.10), channel_id=1, source_target_pairs={{1,0},{2,1},{3,2},{4,3},{5,4},{6,5},{7,6},{8,7},{9,8},{10,9},{11,1... | collective-permute-start | bytes 1572872 | tf_op jit(solution)/shard_map/ppermute | solution.py:26
  309.5 13.5 %collective-permute-start.5 = (bf16[128,2048]{1,0:T(8,128)(2,1)S(1)}, bf16[128,2048]{1,0:T(8,128)(2,1)S(1)}, u32[]{:S(2)}, u32[]{:S(2)}) collective-permute-start(bf16[128,2048]{1,0:T(8,128)(2,1)S(1)} %collective-permute-done.4), channel_id=1, source_target_pairs={{0,1},{1,2},{2,3},{3,4},{4,5},{5,6},{6,7},{7,8},{8,9},{9,10},{10,1... | collective-permute-start | bytes 1572872 | tf_op jit(solution)/shard_map/ppermute | solution.py:24
  310.7 13.5 %collective-permute-start.12 = (bf16[128,2048]{1,0:T(8,128)(2,1)S(1)}, bf16[128,2048]{1,0:T(8,128)(2,1)}, u32[]{:S(2)}, u32[]{:S(2)}) collective-permute-start(bf16[128,2048]{1,0:T(8,128)(2,1)S(1)} %collective-permute-done.11), channel_id=1, source_target_pairs={{1,0},{2,1},{3,2},{4,3},{5,4},{6,5},{7,6},{8,7},{9,8},{10,9},{11,1... | collective-permute-start | bytes 1572872 | tf_op jit(solution)/shard_map/ppermute | solution.py:26
  323.0 14.4 %collective-permute-start.6 = (bf16[128,2048]{1,0:T(8,128)(2,1)S(1)}, bf16[128,2048]{1,0:T(8,128)(2,1)}, u32[]{:S(2)}, u32[]{:S(2)}) collective-permute-start(bf16[128,2048]{1,0:T(8,128)(2,1)S(1)} %collective-permute-done.5), channel_id=1, source_target_pairs={{0,1},{1,2},{2,3},{3,4},{4,5},{5,6},{6,7},{7,8},{8,9},{9,10},{10,1... | collective-permute-start | bytes 1572872 | tf_op jit(solution)/shard_map/ppermute | solution.py:24
  324.1 27.8 %collective-permute-start.13 = (bf16[128,2048]{1,0:T(8,128)(2,1)}, bf16[128,2048]{1,0:T(8,128)(2,1)}, u32[]{:S(2)}, u32[]{:S(2)}) collective-permute-start(bf16[128,2048]{1,0:T(8,128)(2,1)} %collective-permute-done.12), channel_id=1, source_target_pairs={{1,0},{2,1},{3,2},{4,3},{5,4},{6,5},{7,6},{8,7},{9,8},{10,9},{11,1... | collective-permute-start | bytes 1572872 | tf_op jit(solution)/shard_map/ppermute | solution.py:26
  337.4 19.6 %collective-permute-start.7 = (bf16[128,2048]{1,0:T(8,128)(2,1)}, bf16[128,2048]{1,0:T(8,128)(2,1)}, u32[]{:S(2)}, u32[]{:S(2)}) collective-permute-start(bf16[128,2048]{1,0:T(8,128)(2,1)} %collective-permute-done.6), channel_id=1, source_target_pairs={{0,1},{1,2},{2,3},{3,4},{4,5},{5,6},{6,7},{7,8},{8,9},{9,10},{10,1... | collective-permute-start | bytes 1572872 | tf_op jit(solution)/shard_map/ppermute | solution.py:24
  337.4 143.0 %reduce-scatter.2.cloned.1.call-start = ((), (), s32[]{:S(2)}) async-start(), calls=%async_computation.7 | async-start | bytes 8912896 | tf_op jit(solution)/shard_map/reduce_scatter | solution.py:230
  352.0 25.1 %collective-permute-start.14 = (bf16[128,2048]{1,0:T(8,128)(2,1)}, bf16[128,2048]{1,0:T(8,128)(2,1)S(1)}, u32[]{:S(2)}, u32[]{:S(2)}) collective-permute-start(bf16[128,2048]{1,0:T(8,128)(2,1)} %collective-permute-done.13), channel_id=1, source_target_pairs={{1,0},{2,1},{3,2},{4,3},{5,4},{6,5},{7,6},{8,7},{9,8},{10,9},{11,1... | collective-permute-start | bytes 1572872 | tf_op jit(solution)/shard_map/ppermute | solution.py:26
  (27 other events, 913.8 us)
Sparse Core Ops, SparseCore 0:
  239.0 23.3 all-gather.2
  337.5 25.2 all-gather.4
  401.7 78.6 reduce-scatter.1
